TPU v7x, 256 devices: a whole 4x4x8 slice. The times are simulated.
256 devices in a mesh: seq: 16 (over z_lo, x), mp: 16 (over y, z_hi, core).
Axes of the slice: x: 4, y: 4, z: 8 (z_hi: 2, z_lo: 4; z = z_hi * 4 + z_lo), core: 2. Of those that a mesh axis runs over, the one named last changes fastest.
Arguments:
- inputs: bfloat16 [8192, 7168], P('seq')
- norm_gain: float32 [7168], replicated, may hold values from 0.1 to 1.9
- qkv_weight: bfloat16 [7168, 3, 3584], P('seq', None, 'mp'), may hold values from -0.0625 to 0.0625
- adapter_down: bfloat16 [7168, 128], P('seq'), may hold values from -0.0625 to 0.0625
- adapter_up: bfloat16 [3, 128, 3584], P(None, None, 'mp'), may hold values from -0.5 to 0.5
- out_weight: bfloat16 [3584, 3584], P('mp', 'seq'), may hold values from -0.5 to 0.5
- cache_keys: bfloat16 [32, 256, 3584], P('seq', None, 'mp')
- cache_values: bfloat16 [32, 256, 3584], P('seq', None, 'mp'), may hold values from -6 to 6
- cache_lengths: int32 [4], replicated, may hold values from 1 to 2048, 5120 in all
- block_perm: int32 [32], replicated, may hold values from 0 to 31, each once
Outputs:
- block_out: bfloat16 [8192, 3584], P('seq', 'mp')
Inputs may be any that keep to these rules, and one draw needn't show every extreme that they name: `cache_lengths`: each request has at least one cached position, and some request fills all of its 8 blocks. `block_perm`: each logical block appears once.
All inputs are finite; a program needn't handle non-finite values.
Results may differ from a plain program's by a relative error of at most 0.025.
Values may be sent and summed in bfloat16 or wider, within the bound.
A program may use at most 192 MiB of HBM per device.

v0:
```python
import jax
import jax.numpy as jnp
from jax import lax
from jax.sharding import PartitionSpec as P

HD = 224
REQS = 4
QLEN = 2048
lowest = -1e30


def lookup(small_table, positions_of):
    hits = positions_of[..., None] == jnp.arange(small_table.shape[0], dtype=jnp.int32)
    return jnp.sum(jnp.where(hits, small_table, 0), axis=-1)


def query_meta(token_index, lengths):
    request = token_index // QLEN
    return (request, lookup(lengths, request) + token_index % QLEN)


def key_meta(row_index, layout, permutation, lengths):
    cache_rows, block_size, tok_dev, max_blocks = layout
    rows_dev = cache_rows + tok_dev
    device = row_index // rows_dev
    local_row = row_index % rows_dev
    block_index = (
        device * (cache_rows // block_size) + jnp.minimum(local_row, cache_rows - 1) // block_size
    )
    logical = lookup(permutation, block_index)
    request = logical // max_blocks
    position = logical % max_blocks * block_size + local_row % block_size
    cached_live = position < lookup(lengths, request)
    new_req, new_pos = query_meta(device * tok_dev + local_row - cache_rows, lengths)
    in_cache = local_row < cache_rows
    key_req = jnp.where(in_cache, jnp.where(cached_live, request, -1), new_req)
    return (key_req, jnp.where(in_cache, position, new_pos))


def attend(softmax_state, queries, query_info, key_rows, value_rows, key_info, head_dim):
    query_req, query_pos = query_info
    key_req, key_pos = key_info
    visible = (key_req[None, :] == query_req[:, None]) & (key_pos[None, :] <= query_pos[:, None])
    query_count = queries.shape[0]
    key_count = key_rows.shape[0]
    head_count = queries.shape[1] // head_dim
    summed, largest, weight_sum = softmax_state
    scores = jnp.einsum(
        "qhd,khd->hqk",
        queries.reshape(query_count, head_count, head_dim),
        key_rows.reshape(key_count, head_count, head_dim),
        preferred_element_type=jnp.float32,
    ) * head_dim ** (-0.5)
    scores = jnp.where(visible[None], scores, lowest)
    new_largest = jnp.maximum(largest, jnp.max(scores, axis=-1))
    weights = jnp.where(visible[None], jnp.exp(scores - new_largest[..., None]), 0.0)
    weight_sum = jnp.sum(weights, axis=-1)
    summed = jnp.einsum(
        "hqk,khd->hqd",
        weights.astype(jnp.bfloat16),
        value_rows.reshape(key_count, head_count, head_dim),
        preferred_element_type=jnp.float32,
    )
    return (summed, new_largest, weight_sum)


def per_device(
    inputs,
    norm_gain,
    qkv_weight,
    adapter_down,
    adapter_up,
    out_weight,
    cache_keys,
    cache_values,
    cache_lengths,
    block_perm,
):
    tok_dev = inputs.shape[0]
    widened = inputs.astype(jnp.float32)
    normed = (
        widened * lax.rsqrt(jnp.mean(widened * widened, axis=-1, keepdims=True) + 1e-05) * norm_gain
    ).astype(jnp.bfloat16)
    head_width = qkv_weight.shape[2]
    weight_rows = lax.all_gather(qkv_weight, "seq", axis=0, tiled=True)
    down_rows = lax.all_gather(adapter_down, "seq", axis=0, tiled=True)
    main_part = jnp.einsum("tr,rkc->ktc", normed, weight_rows, preferred_element_type=jnp.float32)
    low_rank = jnp.dot(normed, down_rows, preferred_element_type=jnp.float32)
    main_part, low_rank = (main_part, low_rank)
    low_rank = low_rank.astype(jnp.bfloat16)
    projected = (
        main_part
        + jnp.einsum("tr,krc->ktc", low_rank, adapter_up, preferred_element_type=jnp.float32)
    ).astype(jnp.bfloat16)
    queries = projected[0]
    new_keys = projected[1]
    new_values = projected[2]
    cycle_index = lax.axis_index("seq")
    cache_rows = cache_keys.shape[0] * cache_keys.shape[1]
    layout = (cache_rows, cache_keys.shape[1], tok_dev, block_perm.shape[0] // REQS)
    key_rows = jnp.concatenate([cache_keys.reshape(cache_rows, head_width), new_keys], axis=0)
    value_rows = jnp.concatenate([cache_values.reshape(cache_rows, head_width), new_values], axis=0)
    token_ids = jnp.arange(tok_dev, dtype=jnp.int32)
    own_info = query_meta(cycle_index * tok_dev + token_ids, cache_lengths)
    head_count = head_width // HD
    softmax_state = (
        jnp.zeros((head_count, tok_dev, HD), jnp.float32),
        jnp.full((head_count, tok_dev), lowest, jnp.float32),
        jnp.zeros((head_count, tok_dev), jnp.float32),
    )
    pieces = (
        lax.all_gather(key_rows, "seq", axis=0, tiled=True),
        lax.all_gather(value_rows, "seq", axis=0, tiled=True),
    )
    row_ids = jnp.arange(pieces[0].shape[0], dtype=jnp.int32)
    key_info = key_meta(row_ids, layout, block_perm, cache_lengths)
    softmax_state = attend(softmax_state, queries, own_info, pieces[0], pieces[1], key_info, HD)
    summed, largest, weight_sum = softmax_state
    attended = (
        (summed / weight_sum[..., None])
        .transpose(1, 0, 2)
        .reshape(tok_dev, head_width)
        .astype(jnp.bfloat16)
    )
    partial_value = jnp.dot(
        attended,
        lax.all_gather(out_weight, "seq", axis=1, tiled=True),
        preferred_element_type=jnp.float32,
    )
    return lax.psum_scatter(
        partial_value.astype(jnp.bfloat16), "mp", scatter_dimension=1, tiled=True
    )


def solution(mesh):
    in_specs = (
        P("seq", None),
        P(),
        P("seq", None, "mp"),
        P("seq", None),
        P(None, None, "mp"),
        P("mp", "seq"),
        P("seq", None, "mp"),
        P("seq", None, "mp"),
        P(),
        P(),
    )
    out_specs = P("seq", "mp")
    return jax.shard_map(
        per_device, mesh=mesh, in_specs=in_specs, out_specs=out_specs, check_vma=False
    )
```

profile of v0, /device:TPU:2, one launch (start us, length us, event | category | flops | bytes accessed | tf_op | source)
XLA Modules:
  0.0 670.6 jit_solution(3314007942279095606)
XLA Ops:
  6.5 0.7 all-gather.8.cloned.1.call-update
  7.3 0.0 all-gather.6.cloned.1.call-start
  7.3 2.6 copy.19
  9.9 0.0 all-gather.6.cloned.1.call-update
  9.9 0.0 all-gather.10.cloned.1.call-start
  10.0 1.0 copy.24
  11.0 4.6 fusion.5
  15.6 78.8 %all-gather.8.cloned.1.call-done = bf16[7168,128]{1,0:T(8,128)(2,1)} async-done(((bf16[448,128]{1,0:T(8,128)(2,1)}), bf16[7168,128]{1,0:T(8,128)(2,1)}) %all-gather.8.cloned.1.call-update) | async-done | bytes 1835024 | tf_op jit(solution)/shard_map/all_gather | solution.py:86
  94.4 6.3 fusion.16
  100.7 155.4 %all-gather.6.cloned.1.call-done = bf16[7168,3,224]{2,1,0:T(4,128)(2,1)} async-done(((bf16[448,3,224]{2,1,0:T(4,128)(2,1)}), bf16[7168,3,224]{2,1,0:T(4,128)(2,1)}) %all-gather.6.cloned.1.call-update) | async-done | bytes 9633808 | tf_op jit(solution)/shard_map/all_gather | solution.py:85
  256.0 21.6 %copy.20 = bf16[7168,3,224]{0,2,1:T(8,128)(2,1)} copy(bf16[7168,3,224]{2,1,0:T(4,128)(2,1)} %all-gather.6.cloned.1.call-done) | data formatting | bytes 19267584 | tf_op jit(solution)/shard_map/all_gather | solution.py:85
  277.7 10.2 %fusion.10 = f32[512,672]{0,1:S(1)} fusion(bf16[7168,672]{0,1:T(8,128)(2,1)} %bitcast.29, bf16[512,7168]{1,0:T(8,128)(2,1)} %param.10, f32[7168]{0:T(1024)S(1)} %copy-done.6, f32[512]{0:T(512)S(1)} %add_rsqrt_fusion), kind=kOutput, calls=%fused_computation.14 | convolution fusion | flops 4947181568 | bytes 18380800
  287.9 0.4 fusion.24
  288.3 0.8 pad_maximum_fusion
  289.1 0.0 all-gather.12.cloned.1.call-start
  289.2 0.8 pad_maximum_fusion.1
  290.1 0.0 all-gather.14.cloned.1.call-start
  290.1 0.8 copy.23
  290.9 0.2 reduce-scatter.2.cloned.1.call-start
  291.2 0.5 select_reduce_fusion
  291.7 0.1 add_select_fusion.1
  291.8 0.1 select_reduce_fusion.3
  291.9 0.4 select_reduce_fusion.2
  292.3 0.1 select_select_fusion
  292.5 91.8 %all-gather.10.cloned.1.call-done = bf16[16384,224]{0,1:T(8,128)(2,1)} async-done(((bf16[1024,224]{0,1:T(8,128)(2,1)}), bf16[16384,224]{0,1:T(8,128)(2,1)}) %all-gather.10.cloned.1.call-update) | async-done | bytes 7340048 | tf_op jit(solution)/shard_map/all_gather | solution.py:112
  384.3 18.4 %fusion = (f32[512]{0:T(512)S(1)}, f32[512,16384]{1,0:T(8,128)}) fusion(s32[16384]{0:T(1024)S(1)} %get-tuple-element.10, s32[16384]{0:T(1024)S(1)} %get-tuple-element.9, s32[512]{0:T(512)S(1)} %fusion.49, s32[512]{0:T(512)S(1)} %add_select_fusion.9, bf16[16384,224]{0,1:T(8,128)(2,1)} %all-gather.10.cloned.1.call-done, bf16[3,512,224]{1,2,0:T(8,128)(2,1)S(1)} %fusion.24), kind=kOutput, calls=%fused_computation.3 | convolution fusion | flops 3808427520 | bytes 41261056 | tf_op jit(solution)/shard_map/qhd,khd->hqk/dot_general | solution.py:48
  402.7 16.7 %fusion.1 = f32[512]{0:T(512)S(1)} fusion(f32[512,16384]{1,0:T(8,128)} %get-tuple-element.12, f32[512]{0:T(512)S(1)} %broadcast_maximum_fusion, s32[16384]{0:T(1024)S(1)} %get-tuple-element.10, s32[16384]{0:T(1024)S(1)} %get-tuple-element.9, s32[512]{0:T(512)S(1)} %fusion.49, s32[512]{0:T(512)S(1)} %add_select_fusion.9), kind=kLoop, calls=%fused_computation.6 | loop fusion | flops 67108352 | bytes 33693696 | tf_op jit(solution)/shard_map/reduce_sum | solution.py:57
  419.4 59.4 %all-gather.12.cloned.1.call-done = bf16[16384,224]{0,1:T(8,128)(2,1)} async-done(((bf16[1024,224]{0,1:T(8,128)(2,1)}), bf16[16384,224]{0,1:T(8,128)(2,1)}) %all-gather.12.cloned.1.call-update) | async-done | bytes 7340048 | tf_op jit(solution)/shard_map/all_gather | solution.py:113
  478.7 17.6 %fusion.21 = bf16[512,224]{0,1:T(8,128)(2,1)S(1)} fusion(bf16[16384,224]{0,1:T(8,128)(2,1)} %all-gather.12.cloned.1.call-done, f32[512,16384]{1,0:T(8,128)} %get-tuple-element.12, f32[512]{0:T(512)S(1)} %broadcast_maximum_fusion, s32[16384]{0:T(1024)S(1)} %get-tuple-element.10, s32[16384]{0:T(1024)S(1)} %get-tuple-element.9, s32[512]{0:T(512)S(1)} %fusion.49, ...), kind=kOutput, calls=%fused_computation.21 | convolution fusion | flops 3825434624 | bytes 41263104 | tf_op jit(solution)/shard_map/hqk,khd->hqd/dot_general | solution.py:58
  496.3 64.7 %all-gather.14.cloned.1.call-done = bf16[224,3584]{0,1:T(8,128)(2,1)} async-done(((bf16[224,224]{0,1:T(8,128)(2,1)}), bf16[224,3584]{0,1:T(8,128)(2,1)}) %all-gather.14.cloned.1.call-update) | async-done | bytes 1605648 | tf_op jit(solution)/shard_map/all_gather | solution.py:127
  561.0 4.4 convolution_convert_fusion
  565.5 98.3 %reduce-scatter.2.cloned.1.call-done = bf16[512,224]{0,1:T(8,128)(2,1)} async-done(((bf16[512,3584]{0,1:T(8,128)(2,1)}), bf16[512,224]{0,1:T(8,128)(2,1)}) %reduce-scatter.2.cloned.1.call-update) | async-done | bytes 229392 | tf_op jit(solution)/shard_map/reduce_scatter | solution.py:130
  (26 shorter events, 0.2 us)
Async XLA Ops:
  6.5 87.8 %copy-start = (bf16[3,128,224]{1,2,0:T(8,128)(2,1)S(1)}, bf16[3,128,224]{1,2,0:T(8,128)(2,1)}, u32[]{:S(2)}) copy-start(bf16[3,128,224]{1,2,0:T(8,128)(2,1)} %param.14) | copy-start | bytes 516100
  6.5 87.8 %copy-start.6 = (f32[7168]{0:T(1024)S(1)}, f32[7168]{0:T(1024)}, u32[]{:S(2)}) copy-start(f32[7168]{0:T(1024)} %param.11) | copy-start | bytes 86020
  6.5 87.8 %all-gather.8.cloned.1.call-start = ((), (), s32[]{:S(2)}) async-start(), calls=%async_computation.2 | async-start | bytes 1949696 | tf_op jit(solution)/shard_map/all_gather | solution.py:86
  7.3 248.8 %all-gather.6.cloned.1.call-start = ((), (), s32[]{:S(2)}) async-start(), calls=%async_computation.1 | async-start | bytes 15597568 | tf_op jit(solution)/shard_map/all_gather | solution.py:85
  9.9 374.4 %all-gather.10.cloned.1.call-start = ((), (), s32[]{:S(2)}) async-start(), calls=%async_computation.3 | async-start | bytes 7798784 | tf_op jit(solution)/shard_map/all_gather | solution.py:112
  277.7 11.5 %copy-start.2 = (bf16[2,256,224]{1,2,0:T(8,128)(2,1)S(1)}, bf16[2,256,224]{1,2,0:T(8,128)(2,1)}, u32[]{:S(2)}) copy-start(bf16[2,256,224]{1,2,0:T(8,128)(2,1)} %param.17) | copy-start | bytes 688132
  277.7 12.4 %copy-start.3 = (bf16[224,224]{1,0:T(8,128)(2,1)S(1)}, bf16[224,224]{1,0:T(8,128)(2,1)}, u32[]{:S(2)}) copy-start(bf16[224,224]{1,0:T(8,128)(2,1)} %param.15) | copy-start | bytes 301060
  277.7 13.5 %copy-start.5 = (s32[32]{0:T(128)S(1)}, s32[32]{0:T(128)}, u32[]{:S(2)}) copy-start(s32[32]{0:T(128)} %param.19) | copy-start | bytes 388
  277.7 14.1 %copy-start.4 = (s32[4]{0:T(128)S(1)}, s32[4]{0:T(128)}, u32[]{:S(2)}) copy-start(s32[4]{0:T(128)} %param.18) | copy-start | bytes 52
  289.1 189.6 %all-gather.12.cloned.1.call-start = ((), (), s32[]{:S(2)}) async-start(), calls=%async_computation.4 | async-start | bytes 7798784 | tf_op jit(solution)/shard_map/all_gather | solution.py:113
  290.1 270.9 %all-gather.14.cloned.1.call-start = ((), (), s32[]{:S(2)}) async-start(), calls=%async_computation.5 | async-start | bytes 1949696 | tf_op jit(solution)/shard_map/all_gather | solution.py:127
  290.9 372.9 %reduce-scatter.2.cloned.1.call-start = ((), (), s32[]{:S(2)}) async-start(), calls=%async_computation.6 | async-start | bytes 3899392 | tf_op jit(solution)/shard_map/reduce_scatter | solution.py:130
  478.7 185.0 %copy-start.1 = (bf16[3,128,224]{1,2,0:T(8,128)(2,1)S(1)}, bf16[3,128,224]{1,2,0:T(8,128)(2,1)}, u32[]{:S(2)}) copy-start(bf16[3,128,224]{1,2,0:T(8,128)(2,1)} %param.14) | copy-start | bytes 516100
Sparse Core Ops, SparseCore 0:
  9.1 85.1 all-gather.7
  96.2 159.8 all-gather.5
  289.3 95.0 all-gather.9
  386.0 92.7 all-gather.11
  480.4 80.6 all-gather.13
  565.6 98.1 reduce-scatter.1
where the time goes:
time: 672 us; the launch traced here: 671 us
  waiting for transfers between devices  549 us (82%)
  matrix products  56.8 us (8%)
  local copies, waits for them, and re-layouts  26 us (4%)
  other arithmetic  24.6 us (4%)
  between operations  13.6 us (2%)
    all_gather x1, waiting for transfers between devices, per_device(): weight_rows = lax.all_gather(qkv_weight, 'seq', axis=0, tiled=True)  155 us
    reduce_scatter x1, waiting for transfers between devices, per_device(): lax.psum_scatter(partial_value.astype(jnp.bfloat16), 'mp', scatter_dimens...  98.3 us
    all_gather x1, waiting for transfers between devices, per_device(): lax.all_gather(key_rows, 'seq', axis=0, tiled=True)  91.8 us
    all_gather x1, waiting for transfers between devices, per_device(): down_rows = lax.all_gather(adapter_down, 'seq', axis=0, tiled=True)  78.8 us
    all_gather x1, waiting for transfers between devices, per_device(): lax.all_gather(out_weight, 'seq', axis=1, tiled=True)  64.7 us
    all_gather x1, waiting for transfers between devices, per_device(): lax.all_gather(value_rows, 'seq', axis=0, tiled=True)  59.4 us
    all_gather x1, local copies, waits for them, and re-layouts, per_device(): weight_rows = lax.all_gather(qkv_weight, 'seq', axis=0, tiled=True)  21.6 us
    dot_general x1, matrix products, attend(): jnp.einsum('qhd,khd->hqk', queries.reshape(query_count, head_count, head_...  18.4 us
  transfers between devices with their start and end apart: 6, of which 6 were waited for; matrix products, arithmetic and copies ran while one was open for 10% of the time, Pallas kernels for 0%

commit v1 on v0

--- a/solution.py
+++ b/solution.py
@@ -82,7 +82,9 @@
         widened * lax.rsqrt(jnp.mean(widened * widened, axis=-1, keepdims=True) + 1e-05) * norm_gain
     ).astype(jnp.bfloat16)
     head_width = qkv_weight.shape[2]
-    weight_rows = lax.all_gather(qkv_weight, "seq", axis=0, tiled=True)
+    weight_rows = jnp.concatenate(
+        lax.all_to_all(jnp.stack([qkv_weight] * lax.axis_size("seq")), "seq", 0, 0), axis=0
+    )
     down_rows = lax.all_gather(adapter_down, "seq", axis=0, tiled=True)
     main_part = jnp.einsum("tr,rkc->ktc", normed, weight_rows, preferred_element_type=jnp.float32)
     low_rank = jnp.dot(normed, down_rows, preferred_element_type=jnp.float32)

time: 672 us -> 725 us (1.079)
  local copies, waits for them, and re-layouts: 26 us -> 51.1 us
  waiting for transfers between devices: 549 us -> 569 us
  starting transfers between devices: 0.39 us -> 9.24 us
    all_gather x1 -> x0, waiting for transfers between devices: 155 us -> none  [per_device(): weight_rows = lax.all_gather(qkv_weight, 'seq', axis=0, tiled=True)]
    all_gather x1, waiting for transfers between devices: 78.8 us -> 210 us  [per_device(): down_rows = lax.all_gather(adapter_down, 'seq', axis=0, tiled=True)]
    all_gather x1, waiting for transfers between devices: 91.8 us -> 136 us  [per_device(): lax.all_gather(key_rows, 'seq', axis=0, tiled=True)]
    all_to_all x0 -> x1, local copies, waits for them, and re-layouts: none -> 25 us  [per_device(): lax.all_to_all(jnp.stack([qkv_weight] * lax.axis_size('seq')), 'seq', 0, 0)]
    all_gather x1 -> x0, local copies, waits for them, and re-layouts: 21.6 us -> none  [per_device(): weight_rows = lax.all_gather(qkv_weight, 'seq', axis=0, tiled=True)]
    unnamed x16 -> x19, local copies, waits for them, and re-layouts: 3.39 us -> 20.7 us
    all_to_all x0 -> x1, starting transfers between devices: none -> 9.04 us  [per_device(): lax.all_to_all(jnp.stack([qkv_weight] * lax.axis_size('seq')), 'seq', 0, 0)]
  transfers between devices with their start and end apart: 6 -> 6, of which waited for: 6 -> 5; matrix products, arithmetic and copies ran while one was open for 10% -> 9% of each run, Pallas kernels for 0% -> 0%
where the time goes in v1:
time: 725 us
  waiting for transfers between devices  569 us (78%)
  matrix products  56.8 us (8%)
  local copies, waits for them, and re-layouts  51.1 us (7%)
  other arithmetic  24.6 us (3%)
  between operations  13.3 us (2%)
  starting transfers between devices  9.24 us (1%)
    all_gather x1, waiting for transfers between devices, per_device(): down_rows = lax.all_gather(adapter_down, 'seq', axis=0, tiled=True)  210 us
    all_gather x1, waiting for transfers between devices, per_device(): lax.all_gather(key_rows, 'seq', axis=0, tiled=True)  136 us
    reduce_scatter x1, waiting for transfers between devices, per_device(): lax.psum_scatter(partial_value.astype(jnp.bfloat16), 'mp', scatter_dimens...  98.3 us
    all_gather x1, waiting for transfers between devices, per_device(): lax.all_gather(out_weight, 'seq', axis=1, tiled=True)  65 us
    all_gather x1, waiting for transfers between devices, per_device(): lax.all_gather(value_rows, 'seq', axis=0, tiled=True)  59.3 us
    all_to_all x1, local copies, waits for them, and re-layouts, per_device(): lax.all_to_all(jnp.stack([qkv_weight] * lax.axis_size('seq')), 'seq', 0, 0)  25 us
    unnamed x19, local copies, waits for them, and re-layouts  20.7 us
    dot_general x1, matrix products, attend(): jnp.einsum('qhd,khd->hqk', queries.reshape(query_count, head_count, head_...  18.4 us
  transfers between devices with their start and end apart: 6, of which 5 were waited for; matrix products, arithmetic and copies ran while one was open for 9% of the time, Pallas kernels for 0%

profile of v1, /device:TPU:2, one launch (start us, length us, event | category | flops | bytes accessed | tf_op | source)
XLA Modules:
  0.0 724.6 jit_solution(814809283104803685)
XLA Ops:
  6.5 1.4 copy.19
  7.9 5.3 stack.2
  13.3 9.0 %all-to-all-start = ((bf16[16,448,3,224]{1,3,2,0:T(8,128)(2,1)}), bf16[16,448,3,224]{1,3,2,0:T(8,128)(2,1)}, u32[]{:S(2)}, u32[]{:S(2)}) async-start(bf16[16,448,3,224]{1,3,2,0:T(8,128)(2,1)} %stack.2), calls=%async_computation | async-start | bytes 22020096 | tf_op jit(solution)/shard_map/all_to_all | solution.py:86
  22.3 0.0 all-gather.5.cloned.1.call-start
  22.4 0.7 all-gather.5.cloned.1.call-update
  23.1 0.0 all-gather.7.cloned.1.call-start
  23.1 4.6 fusion.5
  27.7 210.2 %all-gather.5.cloned.1.call-done = bf16[7168,128]{1,0:T(8,128)(2,1)} async-done(((bf16[448,128]{1,0:T(8,128)(2,1)}), bf16[7168,128]{1,0:T(8,128)(2,1)}) %all-gather.5.cloned.1.call-update) | async-done | bytes 1835024 | tf_op jit(solution)/shard_map/all_gather | solution.py:88
  238.0 6.3 fusion.16
  244.3 25.0 %copy.20 = bf16[16,448,3,224]{1,0,3,2:T(8,128)(2,1)} copy(bf16[16,448,3,224]{1,3,2,0:T(8,128)(2,1)} %all-to-all-done) | data formatting | bytes 19267584 | tf_op jit(solution)/shard_map/all_to_all | solution.py:86
  269.3 18.6 %reshape.274 = bf16[7168,672]{0,1:T(8,128)(2,1)} reshape(bf16[16,448,3,224]{1,0,3,2:T(8,128)(2,1)} %copy.20) | data formatting | bytes 19267584
  287.9 10.2 %fusion.10 = f32[512,672]{0,1:S(1)} fusion(bf16[7168,672]{0,1:T(8,128)(2,1)} %reshape.274, bf16[512,7168]{1,0:T(8,128)(2,1)} %param.10, f32[7168]{0:T(1024)S(1)} %copy-done.7, f32[512]{0:T(512)S(1)} %add_rsqrt_fusion), kind=kOutput, calls=%fused_computation.14 | convolution fusion | flops 4947181568 | bytes 18380800
  298.0 0.4 fusion.24
  298.5 0.8 pad_maximum_fusion
  299.3 0.0 all-gather.9.cloned.1.call-start
  299.4 0.8 pad_maximum_fusion.1
  300.3 0.0 all-gather.11.cloned.1.call-start
  300.3 0.8 copy.23
  301.1 0.0 reduce-scatter.2.cloned.1.call-start
  301.2 0.5 select_reduce_fusion
  301.7 0.1 add_select_fusion.1
  301.8 0.1 select_reduce_fusion.3
  301.9 0.4 select_reduce_fusion.2
  302.3 0.1 select_select_fusion
  302.5 135.9 %all-gather.7.cloned.1.call-done = bf16[16384,224]{0,1:T(8,128)(2,1)} async-done(((bf16[1024,224]{0,1:T(8,128)(2,1)}), bf16[16384,224]{0,1:T(8,128)(2,1)}) %all-gather.7.cloned.1.call-update) | async-done | bytes 7340048 | tf_op jit(solution)/shard_map/all_gather | solution.py:114
  438.3 18.4 %fusion = (f32[512]{0:T(512)S(1)}, f32[512,16384]{1,0:T(8,128)}) fusion(s32[16384]{0:T(1024)S(1)} %get-tuple-element.10, s32[16384]{0:T(1024)S(1)} %get-tuple-element.9, s32[512]{0:T(512)S(1)} %fusion.49, s32[512]{0:T(512)S(1)} %add_select_fusion.9, bf16[16384,224]{0,1:T(8,128)(2,1)} %all-gather.7.cloned.1.call-done, bf16[3,512,224]{1,2,0:T(8,128)(2,1)S(1)} %fusion.24), kind=kOutput, calls=%fused_computation.3 | convolution fusion | flops 3808427520 | bytes 41261056 | tf_op jit(solution)/shard_map/qhd,khd->hqk/dot_general | solution.py:48
  456.7 16.7 %fusion.1 = f32[512]{0:T(512)S(1)} fusion(f32[512,16384]{1,0:T(8,128)} %get-tuple-element.12, f32[512]{0:T(512)S(1)} %broadcast_maximum_fusion, s32[16384]{0:T(1024)S(1)} %get-tuple-element.10, s32[16384]{0:T(1024)S(1)} %get-tuple-element.9, s32[512]{0:T(512)S(1)} %fusion.49, s32[512]{0:T(512)S(1)} %add_select_fusion.9), kind=kLoop, calls=%fused_computation.6 | loop fusion | flops 67108352 | bytes 33693696 | tf_op jit(solution)/shard_map/reduce_sum | solution.py:57
  473.4 59.3 %all-gather.9.cloned.1.call-done = bf16[16384,224]{0,1:T(8,128)(2,1)} async-done(((bf16[1024,224]{0,1:T(8,128)(2,1)}), bf16[16384,224]{0,1:T(8,128)(2,1)}) %all-gather.9.cloned.1.call-update) | async-done | bytes 7340048 | tf_op jit(solution)/shard_map/all_gather | solution.py:115
  532.8 17.6 %fusion.21 = bf16[512,224]{0,1:T(8,128)(2,1)S(1)} fusion(bf16[16384,224]{0,1:T(8,128)(2,1)} %all-gather.9.cloned.1.call-done, f32[512,16384]{1,0:T(8,128)} %get-tuple-element.12, f32[512]{0:T(512)S(1)} %broadcast_maximum_fusion, s32[16384]{0:T(1024)S(1)} %get-tuple-element.10, s32[16384]{0:T(1024)S(1)} %get-tuple-element.9, s32[512]{0:T(512)S(1)} %fusion.49, ...), kind=kOutput, calls=%fused_computation.21 | convolution fusion | flops 3825434624 | bytes 41263104 | tf_op jit(solution)/shard_map/hqk,khd->hqd/dot_general | solution.py:58
  550.3 65.0 %all-gather.11.cloned.1.call-done = bf16[224,3584]{0,1:T(8,128)(2,1)} async-done(((bf16[224,224]{0,1:T(8,128)(2,1)}), bf16[224,3584]{0,1:T(8,128)(2,1)}) %all-gather.11.cloned.1.call-update) | async-done | bytes 1605648 | tf_op jit(solution)/shard_map/all_gather | solution.py:129
  615.3 4.4 convolution_convert_fusion
  619.7 98.3 %reduce-scatter.2.cloned.1.call-done = bf16[512,224]{0,1:T(8,128)(2,1)} async-done(((bf16[512,3584]{0,1:T(8,128)(2,1)}), bf16[512,224]{0,1:T(8,128)(2,1)}) %reduce-scatter.2.cloned.1.call-update) | async-done | bytes 229392 | tf_op jit(solution)/shard_map/reduce_scatter | solution.py:132
  (29 shorter events, 0.2 us)
Async XLA Ops:
  6.5 231.5 %copy-start = (bf16[3,128,224]{1,2,0:T(8,128)(2,1)S(1)}, bf16[3,128,224]{1,2,0:T(8,128)(2,1)}, u32[]{:S(2)}) copy-start(bf16[3,128,224]{1,2,0:T(8,128)(2,1)} %param.14) | copy-start | bytes 516100
  13.3 9.8 %copy-start.2 = (bf16[2,256,224]{1,2,0:T(8,128)(2,1)S(1)}, bf16[2,256,224]{1,2,0:T(8,128)(2,1)}, u32[]{:S(2)}) copy-start(bf16[2,256,224]{1,2,0:T(8,128)(2,1)} %param.16) | copy-start | bytes 688132
  13.3 224.7 %copy-start.7 = (f32[7168]{0:T(1024)S(1)}, f32[7168]{0:T(1024)}, u32[]{:S(2)}) copy-start(f32[7168]{0:T(1024)} %param.11) | copy-start | bytes 86020
  13.3 231.0 %all-to-all-start = ((bf16[16,448,3,224]{1,3,2,0:T(8,128)(2,1)}), bf16[16,448,3,224]{1,3,2,0:T(8,128)(2,1)}, u32[]{:S(2)}, u32[]{:S(2)}) async-start(bf16[16,448,3,224]{1,3,2,0:T(8,128)(2,1)} %stack.2), calls=%async_computation | async-start | bytes 22020096 | tf_op jit(solution)/shard_map/all_to_all | solution.py:86
  22.3 215.7 %all-gather.5.cloned.1.call-start = ((), (), s32[]{:S(2)}) async-start(), calls=%async_computation.2 | async-start | bytes 1949696 | tf_op jit(solution)/shard_map/all_gather | solution.py:88
  23.1 415.3 %all-gather.7.cloned.1.call-start = ((), (), s32[]{:S(2)}) async-start(), calls=%async_computation.3 | async-start | bytes 7798784 | tf_op jit(solution)/shard_map/all_gather | solution.py:114
  287.9 11.5 %copy-start.3 = (bf16[2,256,224]{1,2,0:T(8,128)(2,1)S(1)}, bf16[2,256,224]{1,2,0:T(8,128)(2,1)}, u32[]{:S(2)}) copy-start(bf16[2,256,224]{1,2,0:T(8,128)(2,1)} %param.17) | copy-start | bytes 688132
  287.9 12.5 %copy-start.4 = (bf16[224,224]{1,0:T(8,128)(2,1)S(1)}, bf16[224,224]{1,0:T(8,128)(2,1)}, u32[]{:S(2)}) copy-start(bf16[224,224]{1,0:T(8,128)(2,1)} %param.15) | copy-start | bytes 301060
  287.9 13.3 %copy-start.6 = (s32[32]{0:T(128)S(1)}, s32[32]{0:T(128)}, u32[]{:S(2)}) copy-start(s32[32]{0:T(128)} %param.19) | copy-start | bytes 388
  287.9 13.9 %copy-start.5 = (s32[4]{0:T(128)S(1)}, s32[4]{0:T(128)}, u32[]{:S(2)}) copy-start(s32[4]{0:T(128)} %param.18) | copy-start | bytes 52
  299.3 233.4 %all-gather.9.cloned.1.call-start = ((), (), s32[]{:S(2)}) async-start(), calls=%async_computation.4 | async-start | bytes 7798784 | tf_op jit(solution)/shard_map/all_gather | solution.py:115
  300.3 315.1 %all-gather.11.cloned.1.call-start = ((), (), s32[]{:S(2)}) async-start(), calls=%async_computation.5 | async-start | bytes 1949696 | tf_op jit(solution)/shard_map/all_gather | solution.py:129
  301.1 416.9 %reduce-scatter.2.cloned.1.call-start = ((), (), s32[]{:S(2)}) async-start(), calls=%async_computation.6 | async-start | bytes 3899392 | tf_op jit(solution)/shard_map/reduce_scatter | solution.py:132
  532.8 185.3 %copy-start.1 = (bf16[3,128,224]{1,2,0:T(8,128)(2,1)S(1)}, bf16[3,128,224]{1,2,0:T(8,128)(2,1)}, u32[]{:S(2)}) copy-start(bf16[3,128,224]{1,2,0:T(8,128)(2,1)} %param.14) | copy-start | bytes 516100
Sparse Core Ops, SparseCore 0:
  24.9 213.0 all-gather.4
  299.4 138.8 all-gather.6
  440.1 92.5 all-gather.8
  534.4 80.8 all-gather.10
  619.9 98.1 reduce-scatter.1
